TPU v7x, 256 devices: a whole 4x4x8 slice. The times are simulated.
256 devices in a mesh: cluster: 8 (over z), sub: 32 (over x, y, core).
Axes of the slice: x: 4, y: 4, z: 8, core: 2. Of those that a mesh axis runs over, the one named last changes fastest.
Arguments:
- dual_ops: bfloat16 [8, 32, 2048, 2048], P('cluster', 'sub'), as said below
- corner_coupling: float32 [8, 32, 48, 2048], P('cluster', 'sub'), may hold values from -0.3 to 0.3
- coarse_inverse: float32 [32, 128, 128], P('sub'), as said below
- corner_map: int32 [8, 32, 48], P('cluster', 'sub'), may hold values from 0 to 127, as said below
- interface_tiles: int32 [8, 32, 4], P('cluster', 'sub'), may hold values from 1 to 4, as said below
- gap_terms: float32 [8, 32, 2048, 128], P('cluster', 'sub')
Outputs:
- multipliers: float32 [8, 32, 2048, 128], P('cluster', 'sub')
- residual: float32 [8, 32, 2048, 128], P('cluster', 'sub')
Inputs may be any that keep to these rules, and one draw needn't show every extreme that they name: interface_tiles[c, s, k] counts the tiles that subdomain (c, s) shares with the subdomain at sub distance -2, -1, +1, +2 for k = 0..3, wrapping around 32; the count for distance +d equals that neighbour's count for distance -d; in every c some subdomain has 4 for all four. `corner_map`: the 48 entries of one subdomain are distinct. `dual_ops`: each matrix is symmetric positive definite. `coarse_inverse`: each matrix is symmetric positive definite.
All inputs are finite; a program needn't handle non-finite values.
Results may differ from a plain program's by a relative error of at most 0.009.
Values sent between devices are 32-bit elements; how exact they have to be, the bound alone decides.
No kernel may reach another device: no remote copies, remote signals or barrier semaphores. Data moves between devices by JAX's collectives and lax.ppermute only.
A program may use at most 64 MiB of HBM per device.

v0:
```python
import jax
import jax.numpy as jnp
from jax import lax
from jax.sharding import PartitionSpec as P

TILE = 128
MAXT = 4
NCOARSE = 128
ITERS = 3


def passed_along(block, axis, distance):
    devices = range(lax.axis_size(axis))
    route = [((i - distance) % len(devices), i) for i in devices]
    return lax.ppermute(block, axis, route)


def extract_run(values_in, start_row, row_count):
    run_rows = MAXT * TILE
    run_block = lax.dynamic_slice_in_dim(values_in, start_row, run_rows, 0)
    keep_mask = jnp.arange(run_rows, dtype=jnp.int32)[:, None] < row_count
    return jnp.where(keep_mask, run_block, jnp.zeros_like(run_block))


def insert_run(run_block, start_row, dual_rows):
    padded = jnp.zeros((dual_rows + run_block.shape[0], run_block.shape[1]), run_block.dtype)
    return lax.dynamic_update_slice_in_dim(padded, run_block, start_row, 0)[:dual_rows]


def local(dual_ops, corner_coupling, coarse_inverse, corner_map, interface_tiles, gap_terms):
    highest = lax.Precision.HIGHEST
    operator = dual_ops[0, 0]
    coupling = corner_coupling[0, 0]
    inverse = coarse_inverse[0]
    corners = corner_map[0, 0]
    lengths = interface_tiles[0, 0] * TILE
    run_start = jnp.concatenate([jnp.zeros((1,), jnp.int32), jnp.cumsum(lengths)[:3]])
    dual_rows = operator.shape[0]
    live_mask = jnp.arange(dual_rows, dtype=jnp.int32)[:, None] < jnp.sum(lengths)
    onehot = (corners[:, None] == jnp.arange(NCOARSE, dtype=jnp.int32)[None, :]).astype(jnp.float32)

    def assemble(values_in):
        incoming = [None, None, None, None]
        for run_index, distance in enumerate((-2, -1, 1, 2)):
            outgoing = extract_run(values_in, run_start[3 - run_index], lengths[3 - run_index])
            incoming[run_index] = passed_along(outgoing, "sub", -distance)
        assembled = jnp.where(live_mask, values_in, jnp.zeros_like(values_in))
        for run_index in range(4):
            assembled = assembled + insert_run(incoming[run_index], run_start[run_index], dual_rows)
        return assembled

    residual = assemble(gap_terms[0, 0])
    direction = residual
    multipliers = jnp.zeros_like(residual)
    norm_now = lax.psum(jnp.sum(residual * residual, axis=0), ("cluster", "sub"))
    for iteration in range(ITERS):
        local_part = jnp.dot(
            operator, direction.astype(jnp.bfloat16), preferred_element_type=jnp.float32
        )
        corner_values = jnp.dot(coupling, direction, precision=highest)
        coarse_part = jnp.dot(onehot.T, corner_values, precision=highest)
        coarse_total = lax.psum(coarse_part, "cluster")
        coarse_solution = jnp.dot(inverse, coarse_total, precision=highest)
        corner_back = jnp.dot(onehot, coarse_solution, precision=highest)
        image = assemble(local_part + jnp.dot(coupling.T, corner_back, precision=highest))
        curvature = lax.psum(jnp.sum(direction * image, axis=0), ("cluster", "sub"))
        step_size = norm_now / curvature
        multipliers = multipliers + step_size * direction
        residual = residual - step_size * image
        norm_next = lax.psum(jnp.sum(residual * residual, axis=0), ("cluster", "sub"))
        direction = residual + norm_next / norm_now * direction
        norm_now = norm_next
    return (multipliers[None, None], residual[None, None])


def solution(mesh):
    in_specs = (
        P("cluster", "sub", None, None),
        P("cluster", "sub", None, None),
        P("sub", None, None),
        P("cluster", "sub", None),
        P("cluster", "sub", None),
        P("cluster", "sub", None, None),
    )
    out_specs = (P("cluster", "sub", None, None), P("cluster", "sub", None, None))
    return jax.shard_map(local, mesh=mesh, in_specs=in_specs, out_specs=out_specs, check_vma=False)
```

profile of v0, /device:TPU:1, one launch (start us, length us, event | category | flops | bytes accessed | tf_op | source)
XLA Modules:
  0.0 746.1 jit_solution(15423645180526299071)
XLA Ops:
  7.2 1.3 fusion.62
  14.9 1.2 constant_dynamic-slice_fusion.1
  16.8 1.2 iota_compare_fusion.6
  18.1 2.8 collective-permute-start.1
  22.6 4.8 collective-permute-start.3
  32.6 1.2 broadcast.85.clone.2
  33.8 1.8 dynamic_update_slice.49
  35.6 1.2 broadcast.85.clone.1
  36.9 1.9 dynamic_update_slice.50
  38.8 1.2 broadcast.85.clone
  40.0 1.8 dynamic_update_slice.51
  41.8 2.2 fusion.12
  46.0 70.0 %all-reduce.9.cloned.1.call-done = f32[128,128]{1,0:T(8,128)} async-done(((f32[128,128]{1,0:T(8,128)}), f32[128,128]{1,0:T(8,128)}) %all-reduce.9.cloned.1.call-update) | async-done | bytes 65552 | tf_op jit(solution)/shard_map/psum | solution.py:62
  116.0 1.1 fusion.43
  118.4 6.3 fusion.6
  125.8 6.7 collective-permute-start.5
  132.6 4.1 collective-permute-start.7
  136.7 1.2 broadcast.85.clone.5
  137.9 1.8 dynamic_update_slice.53
  139.7 1.4 collective-permute-done.6
  141.1 1.2 broadcast.85.clone.4
  142.3 1.9 dynamic_update_slice.54
  144.2 1.2 broadcast.85.clone.3
  145.4 1.8 dynamic_update_slice.55
  147.2 2.8 multiply_reduce_fusion.4
  150.0 78.7 %all-reduce.4 = (f32[128]{0:T(128)S(1)}, f32[128]{0:T(128)S(1)}) all-reduce(f32[128]{0:T(128)} %get-tuple-element.5, f32[128]{0:T(128)} %get-tuple-element.4), channel_id=1, replica_groups=mesh['cluster'=8,'sub'=32] {'cluster','sub'}, use_global_device_ids=true, to_apply=%region_3.4 | all-reduce | flops 256 | bytes 2048 | tf_op jit(solution)/shard_map/psum | solution.py:55
  229.6 72.4 %psum.66 = f32[128]{0:T(128)S(1)} all-reduce(f32[128]{0:T(128)S(1)} %multiply_reduce_fusion.3), channel_id=1, replica_groups=mesh['cluster'=8,'sub'=32] {'cluster','sub'}, use_global_device_ids=true, to_apply=%region_8.9 | all-reduce | flops 128 | bytes 1024 | tf_op jit(solution)/shard_map/psum | solution.py:70
  305.5 7.2 fusion.2
  312.7 56.5 %all-reduce.11.cloned.1.call-done = f32[128,128]{1,0:T(8,128)} async-done(((f32[128,128]{1,0:T(8,128)}), f32[128,128]{1,0:T(8,128)}) %all-reduce.11.cloned.1.call-update) | async-done | bytes 65552 | tf_op jit(solution)/shard_map/psum | solution.py:62
  369.3 1.2 fusion.41
  370.6 2.3 convolution_add_fusion.1
  374.1 6.7 collective-permute-start.9
  381.5 3.6 collective-permute-start.11
  385.3 1.2 broadcast.85.clone.8
  386.5 1.9 dynamic_update_slice.57
  388.4 1.2 collective-permute-done.10
  389.6 1.2 broadcast.85.clone.7
  390.8 1.9 dynamic_update_slice.58
  392.7 1.2 broadcast.85.clone.6
  393.9 1.9 dynamic_update_slice.59
  395.8 4.2 multiply_reduce_fusion.2
  400.0 78.7 %psum.68 = f32[128]{0:T(128)} all-reduce(f32[128]{0:T(128)} %get-tuple-element.12), channel_id=1, replica_groups=mesh['cluster'=8,'sub'=32] {'cluster','sub'}, use_global_device_ids=true, to_apply=%region_11.12 | all-reduce | flops 128 | bytes 1024 | tf_op jit(solution)/shard_map/psum | solution.py:66
  479.3 3.0 multiply_reduce_fusion.1
  482.3 72.5 %psum.69 = f32[128]{0:T(128)S(1)} all-reduce(f32[128]{0:T(128)} %get-tuple-element.10), channel_id=1, replica_groups=mesh['cluster'=8,'sub'=32] {'cluster','sub'}, use_global_device_ids=true, to_apply=%region_13.14 | all-reduce | flops 128 | bytes 1024 | tf_op jit(solution)/shard_map/psum | solution.py:70
  555.4 1.4 multiply_add_fusion
  558.7 7.2 fusion
  565.9 56.7 %all-reduce.13.cloned.1.call-done = f32[128,128]{1,0:T(8,128)} async-done(((f32[128,128]{1,0:T(8,128)}), f32[128,128]{1,0:T(8,128)}) %all-reduce.13.cloned.1.call-update) | async-done | bytes 65552 | tf_op jit(solution)/shard_map/psum | solution.py:62
  622.6 1.2 fusion.39
  624.0 2.3 convolution_add_fusion
  626.3 1.1 select_bitcast_fusion.2
  627.4 6.7 collective-permute-start.13
  634.9 3.6 collective-permute-start.15
  638.7 1.2 broadcast.85.clone.11
  639.9 1.9 dynamic_update_slice.61
  641.8 1.1 collective-permute-done.14
  642.9 1.2 broadcast.85.clone.10
  644.1 1.9 dynamic_update_slice.62
  646.0 1.2 broadcast.85.clone.9
  647.2 1.9 dynamic_update_slice.63
  649.1 3.7 multiply_reduce_fusion
  652.8 78.6 %psum.71 = f32[128]{0:T(128)} all-reduce(f32[128]{0:T(128)S(1)} %get-tuple-element.8), channel_id=1, replica_groups=mesh['cluster'=8,'sub'=32] {'cluster','sub'}, use_global_device_ids=true, to_apply=%region_16.17 | all-reduce | flops 128 | bytes 1024 | tf_op jit(solution)/shard_map/psum | solution.py:66
  732.1 3.3 subtract_bitcast_fusion
  735.4 2.6 copy.13
  738.0 1.3 copy.14
  (105 shorter events, 20.7 us)
Async XLA Ops:
  7.2 36.8 %copy-start = (f32[1,1,48,2048]{3,2,1,0:T(8,128)S(1)}, f32[1,1,48,2048]{3,2,1,0:T(8,128)}, u32[]{:S(2)}) copy-start(f32[1,1,48,2048]{3,2,1,0:T(8,128)} %param.7) | copy-start | bytes 1179652
  7.2 108.8 %all-reduce.9.cloned.1.call-start = ((), (), s32[]{:S(2)}) async-start(), calls=%async_computation | async-start | bytes 131072 | tf_op jit(solution)/shard_map/psum | solution.py:62
  16.1 5.5 copy-start.4
  18.1 14.6 %collective-permute-start.1 = (f32[512,128]{0,1:T(8,128)S(1)}, f32[512,128]{0,1:T(8,128)S(1)}, u32[]{:S(2)}, u32[]{:S(2)}) collective-permute-start(f32[512,128]{0,1:T(8,128)S(1)} %bitcast_select_fusion.2), channel_id=1, source_target_pairs={{31,0},{0,1},{1,2},{2,3},{3,4},{4,5},{5,6},{6,7},{7,8},{8,9},{9,10... | collective-permute-start | bytes 786440 | tf_op jit(solution)/shard_map/ppermute | solution.py:15
  21.0 14.7 %collective-permute-start.2 = (f32[512,128]{0,1:T(8,128)S(1)}, f32[512,128]{0,1:T(8,128)}, u32[]{:S(2)}, u32[]{:S(2)}) collective-permute-start(f32[512,128]{0,1:T(8,128)S(1)} %bitcast_select_fusion.1), channel_id=1, source_target_pairs={{1,0},{2,1},{3,2},{4,3},{5,4},{6,5},{7,6},{8,7},{9,8},{10,9},{11,1... | collective-permute-start | bytes 786440 | tf_op jit(solution)/shard_map/ppermute | solution.py:15
  22.6 9.4 %copy-start.7 = (pred[512]{0:T(512)(128)(4,1)}, pred[512]{0:T(512)(128)(4,1)S(1)}, u32[]{:S(2)}) copy-start(pred[512]{0:T(512)(128)(4,1)S(1)} %iota_compare_fusion.5) | copy-start | bytes 1540
  22.6 16.2 %collective-permute-start.3 = (f32[512,128]{0,1:T(8,128)S(1)}, f32[512,128]{0,1:T(8,128)S(1)}, u32[]{:S(2)}, u32[]{:S(2)}) collective-permute-start(f32[512,128]{0,1:T(8,128)S(1)} %fusion.38), channel_id=1, source_target_pairs={{2,0},{3,1},{4,2},{5,3},{6,4},{7,5},{8,6},{9,7},{10,8},{11,9},{12,... | collective-permute-start | bytes 786440 | tf_op jit(solution)/shard_map/ppermute | solution.py:15
  28.1 8.7 %copy-start.11 = (pred[512]{0:T(512)(128)(4,1)}, pred[512]{0:T(512)(128)(4,1)S(1)}, u32[]{:S(2)}) copy-start(pred[512]{0:T(512)(128)(4,1)S(1)} %iota_compare_fusion.8) | copy-start | bytes 1540
  28.2 13.6 %collective-permute-start = (f32[512,128]{0,1:T(8,128)S(1)}, f32[512,128]{0,1:T(8,128)S(1)}, u32[]{:S(2)}, u32[]{:S(2)}) collective-permute-start(f32[512,128]{0,1:T(8,128)S(1)} %bitcast_select_fusion.3), channel_id=1, source_target_pairs={{30,0},{31,1},{0,2},{1,3},{2,4},{3,5},{4,6},{5,7},{6,8},{7,9},{8,1... | collective-permute-start | bytes 786440 | tf_op jit(solution)/shard_map/ppermute | solution.py:15
  44.0 1.0 copy-start.6
  44.0 72.0 %copy-start.5 = (f32[1,128,128]{2,1,0:T(8,128)S(1)}, f32[1,128,128]{2,1,0:T(8,128)}, u32[]{:S(2)}) copy-start(f32[1,128,128]{2,1,0:T(8,128)} %param.8) | copy-start | bytes 196612
  45.9 323.3 %all-reduce.11.cloned.1.call-start = ((), (), s32[]{:S(2)}) async-start(), calls=%async_computation.1 | async-start | bytes 131072 | tf_op jit(solution)/shard_map/psum | solution.py:62
  118.4 6.3 copy-start.12
  124.7 7.8 %copy-start.8 = (pred[512]{0:T(512)(128)(4,1)S(1)}, pred[512]{0:T(512)(128)(4,1)}, u32[]{:S(2)}) copy-start(pred[512]{0:T(512)(128)(4,1)} %copy-done.7) | copy-start | bytes 1540
  125.8 10.9 %collective-permute-start.5 = (f32[512,128]{0,1:T(8,128)S(1)}, f32[512,128]{0,1:T(8,128)S(1)}, u32[]{:S(2)}, u32[]{:S(2)}) collective-permute-start(f32[512,128]{0,1:T(8,128)S(1)} %get-tuple-element.23), channel_id=1, source_target_pairs={{31,0},{0,1},{1,2},{2,3},{3,4},{4,5},{5,6},{6,7},{7,8},{8,9},{9,10... | collective-permute-start | bytes 786440 | tf_op jit(solution)/shard_map/ppermute | solution.py:15
  132.5 8.6 %collective-permute-start.6 = (f32[512,128]{0,1:T(8,128)}, f32[512,128]{0,1:T(8,128)S(1)}, u32[]{:S(2)}, u32[]{:S(2)}) collective-permute-start(f32[512,128]{0,1:T(8,128)} %get-tuple-element.22), channel_id=1, source_target_pairs={{1,0},{2,1},{3,2},{4,3},{5,4},{6,5},{7,6},{8,7},{9,8},{10,9},{11,1... | collective-permute-start | bytes 786440 | tf_op jit(solution)/shard_map/ppermute | solution.py:15
  132.6 11.6 %collective-permute-start.7 = (f32[512,128]{0,1:T(8,128)S(1)}, f32[512,128]{0,1:T(8,128)S(1)}, u32[]{:S(2)}, u32[]{:S(2)}) collective-permute-start(f32[512,128]{0,1:T(8,128)S(1)} %slice_select_fusion.2), channel_id=1, source_target_pairs={{2,0},{3,1},{4,2},{5,3},{6,4},{7,5},{8,6},{9,7},{10,8},{11,9},{12,... | collective-permute-start | bytes 786440 | tf_op jit(solution)/shard_map/ppermute | solution.py:15
  136.7 10.5 %collective-permute-start.4 = (f32[512,128]{0,1:T(8,128)}, f32[512,128]{0,1:T(8,128)}, u32[]{:S(2)}, u32[]{:S(2)}) collective-permute-start(f32[512,128]{0,1:T(8,128)} %get-tuple-element.21), channel_id=1, source_target_pairs={{30,0},{31,1},{0,2},{1,3},{2,4},{3,5},{4,6},{5,7},{6,8},{7,9},{8,1... | collective-permute-start | bytes 786440 | tf_op jit(solution)/shard_map/ppermute | solution.py:15
  228.7 0.6 copy-start.15
  302.0 0.5 copy-start.20
  305.5 317.1 %all-reduce.13.cloned.1.call-start = ((), (), s32[]{:S(2)}) async-start(), calls=%async_computation.2 | async-start | bytes 131072 | tf_op jit(solution)/shard_map/psum | solution.py:62
  370.4 2.5 copy-start.13
  372.9 7.9 %copy-start.2 = (f32[128,2048]{1,0:T(8,128)}, f32[128,2048]{1,0:T(8,128)S(1)}, u32[]{:S(2)}) copy-start(f32[128,2048]{1,0:T(8,128)S(1)} %convolution_add_fusion.1) | copy-start | bytes 3145732
  373.0 7.9 %copy-start.9 = (pred[512]{0:T(512)(128)(4,1)S(1)}, pred[512]{0:T(512)(128)(4,1)}, u32[]{:S(2)}) copy-start(pred[512]{0:T(512)(128)(4,1)} %copy-done.7) | copy-start | bytes 1540
  374.1 11.2 %collective-permute-start.9 = (f32[512,128]{0,1:T(8,128)S(1)}, f32[512,128]{0,1:T(8,128)}, u32[]{:S(2)}, u32[]{:S(2)}) collective-permute-start(f32[512,128]{0,1:T(8,128)S(1)} %get-tuple-element.20), channel_id=1, source_target_pairs={{31,0},{0,1},{1,2},{2,3},{3,4},{4,5},{5,6},{6,7},{7,8},{8,9},{9,10... | collective-permute-start | bytes 786440 | tf_op jit(solution)/shard_map/ppermute | solution.py:15
  380.8 8.8 %collective-permute-start.10 = (f32[512,128]{0,1:T(8,128)}, f32[512,128]{0,1:T(8,128)}, u32[]{:S(2)}, u32[]{:S(2)}) collective-permute-start(f32[512,128]{0,1:T(8,128)} %get-tuple-element.19), channel_id=1, source_target_pairs={{1,0},{2,1},{3,2},{4,3},{5,4},{6,5},{7,6},{8,7},{9,8},{10,9},{11,1... | collective-permute-start | bytes 786440 | tf_op jit(solution)/shard_map/ppermute | solution.py:15
  381.5 11.1 %collective-permute-start.11 = (f32[512,128]{0,1:T(8,128)}, f32[512,128]{0,1:T(8,128)}, u32[]{:S(2)}, u32[]{:S(2)}) collective-permute-start(f32[512,128]{0,1:T(8,128)} %slice_select_fusion.1), channel_id=1, source_target_pairs={{2,0},{3,1},{4,2},{5,3},{6,4},{7,5},{8,6},{9,7},{10,8},{11,9},{12,... | collective-permute-start | bytes 786440 | tf_op jit(solution)/shard_map/ppermute | solution.py:15
  385.1 10.7 %collective-permute-start.8 = (f32[512,128]{0,1:T(8,128)}, f32[512,128]{0,1:T(8,128)}, u32[]{:S(2)}, u32[]{:S(2)}) collective-permute-start(f32[512,128]{0,1:T(8,128)} %get-tuple-element.18), channel_id=1, source_target_pairs={{30,0},{31,1},{0,2},{1,3},{2,4},{3,5},{4,6},{5,7},{6,8},{7,9},{8,1... | collective-permute-start | bytes 786440 | tf_op jit(solution)/shard_map/ppermute | solution.py:15
  479.3 3.0 copy-start.17
  554.8 0.6 copy-start.19
  623.8 2.5 copy-start.14
  626.3 7.9 %copy-start.1 = (f32[128,2048]{1,0:T(8,128)}, f32[128,2048]{1,0:T(8,128)S(1)}, u32[]{:S(2)}) copy-start(f32[128,2048]{1,0:T(8,128)S(1)} %convolution_add_fusion) | copy-start | bytes 3145732
  626.3 7.9 %copy-start.10 = (pred[512]{0:T(512)(128)(4,1)S(1)}, pred[512]{0:T(512)(128)(4,1)}, u32[]{:S(2)}) copy-start(pred[512]{0:T(512)(128)(4,1)} %copy-done.7) | copy-start | bytes 1540
  627.4 11.3 %collective-permute-start.13 = (f32[512,128]{0,1:T(8,128)S(1)}, f32[512,128]{0,1:T(8,128)}, u32[]{:S(2)}, u32[]{:S(2)}) collective-permute-start(f32[512,128]{0,1:T(8,128)S(1)} %get-tuple-element.17), channel_id=1, source_target_pairs={{31,0},{0,1},{1,2},{2,3},{3,4},{4,5},{5,6},{6,7},{7,8},{8,9},{9,10... | collective-permute-start | bytes 786440 | tf_op jit(solution)/shard_map/ppermute | solution.py:15
  634.1 8.7 %collective-permute-start.14 = (f32[512,128]{0,1:T(8,128)}, f32[512,128]{0,1:T(8,128)}, u32[]{:S(2)}, u32[]{:S(2)}) collective-permute-start(f32[512,128]{0,1:T(8,128)} %get-tuple-element.16), channel_id=1, source_target_pairs={{1,0},{2,1},{3,2},{4,3},{5,4},{6,5},{7,6},{8,7},{9,8},{10,9},{11,1... | collective-permute-start | bytes 786440 | tf_op jit(solution)/shard_map/ppermute | solution.py:15
  634.9 11.1 %collective-permute-start.15 = (f32[512,128]{0,1:T(8,128)}, f32[512,128]{0,1:T(8,128)}, u32[]{:S(2)}, u32[]{:S(2)}) collective-permute-start(f32[512,128]{0,1:T(8,128)} %slice_select_fusion), channel_id=1, source_target_pairs={{2,0},{3,1},{4,2},{5,3},{6,4},{7,5},{8,6},{9,7},{10,8},{11,9},{12,... | collective-permute-start | bytes 786440 | tf_op jit(solution)/shard_map/ppermute | solution.py:15
  638.5 10.7 %collective-permute-start.12 = (f32[512,128]{0,1:T(8,128)}, f32[512,128]{0,1:T(8,128)}, u32[]{:S(2)}, u32[]{:S(2)}) collective-permute-start(f32[512,128]{0,1:T(8,128)} %get-tuple-element.15), channel_id=1, source_target_pairs={{30,0},{31,1},{0,2},{1,3},{2,4},{3,5},{4,6},{5,7},{6,8},{7,9},{8,1... | collective-permute-start | bytes 786440 | tf_op jit(solution)/shard_map/ppermute | solution.py:15
  649.1 83.0 %copy-start.16 = (f32[128]{0:T(128)S(1)}, f32[128]{0:T(128)}, u32[]{:S(2)}) copy-start(f32[128]{0:T(128)} %copy-done.15) | copy-start | bytes 1540
  649.1 83.0 %copy-start.18 = (f32[128]{0:T(128)S(1)}, f32[128]{0:T(128)}, u32[]{:S(2)}) copy-start(f32[128]{0:T(128)} %copy-done.17) | copy-start | bytes 1540
  735.4 2.6 copy-start.3
Sparse Core Ops, SparseCore 0:
  46.1 69.9 all-reduce.8
  305.6 63.6 all-reduce.10
  558.8 63.7 all-reduce.12
where the time goes:
time: 756 us; the launch traced here: 746 us
  blocking collectives  381 us (50%)
  waiting for transfers between devices  187 us (25%)
  local copies, waits for them, and re-layouts  45.1 us (6%)
  starting transfers between devices  40.2 us (5%)
  matrix products  36 us (5%)
  other arithmetic  33.2 us (4%)
  between operations  23.7 us (3%)
    psum x3, blocking collectives, local(): lax.psum(jnp.sum(residual * residual, axis=0), ('cluster', 'sub'))  224 us
    psum x3, waiting for transfers between devices, local(): coarse_total = lax.psum(coarse_part, 'cluster')  183 us
    psum x2, blocking collectives, local(): curvature = lax.psum(jnp.sum(direction * image, axis=0), ('cluster', 'sub'))  157 us
    ppermute x16, starting transfers between devices, passed_along(): return lax.ppermute(block, axis, route)  40 us
    dynamic_update_slice x12, local copies, waits for them, and re-layouts, insert_run(): lax.dynamic_update_slice_in_dim(padded, run_block, start_row, 0)[:dual_rows]  22.4 us
    dot_general x3, matrix products, local(): jnp.dot(operator, direction.astype(jnp.bfloat16), preferred_element_type=...  20.7 us
  transfers between devices with their start and end apart: 19, of which 6 were waited for; matrix products, arithmetic and copies ran while one was open for 7% of the time, Pallas kernels for 0%

commit v1 on v0

--- a/solution.py
+++ b/solution.py
@@ -7,6 +7,15 @@
 MAXT = 4
 NCOARSE = 128
 ITERS = 3
+
+
+def added_up(shard, name):
+    size = lax.axis_size(name)
+    total, hop = (shard, 1)
+    while hop < size:
+        total = total + lax.ppermute(total, name, [(i, i ^ hop) for i in range(size)])
+        hop = 2 * hop
+    return total
 
 
 def passed_along(block, axis, distance):
@@ -59,7 +68,7 @@
         )
         corner_values = jnp.dot(coupling, direction, precision=highest)
         coarse_part = jnp.dot(onehot.T, corner_values, precision=highest)
-        coarse_total = lax.psum(coarse_part, "cluster")
+        coarse_total = added_up(coarse_part, "cluster")
         coarse_solution = jnp.dot(inverse, coarse_total, precision=highest)
         corner_back = jnp.dot(onehot, coarse_solution, precision=highest)
         image = assemble(local_part + jnp.dot(coupling.T, corner_back, precision=highest))

time: 756 us -> 586 us (0.78)
  waiting for transfers between devices: 187 us -> 23.5 us
  between operations: 23.7 us -> 11.2 us
  starting transfers between devices: 40.2 us -> 52 us
  matrix products: 36 us -> 27.2 us
    psum x3 -> x0, waiting for transfers between devices: 183 us -> none  [local(): coarse_total = lax.psum(coarse_part, 'cluster')]
    ppermute x0 -> x9, waiting for transfers between devices: none -> 19.3 us  [added_up(): lax.ppermute(total, name, [(i, i ^ hop) for i in range(size)])]
    ppermute x0 -> x9, starting transfers between devices: none -> 17.1 us  [added_up(): lax.ppermute(total, name, [(i, i ^ hop) for i in range(size)])]
  transfers between devices with their start and end apart: 19 -> 25, of which waited for: 6 -> 13; matrix products, arithmetic and copies ran while one was open for 7% -> 9% of each run, Pallas kernels for 0% -> 0%
where the time goes in v1:
time: 586 us; the launch traced here: 576 us
  blocking collectives  383 us (65%)
  starting transfers between devices  52 us (9%)
  local copies, waits for them, and re-layouts  45.1 us (8%)
  other arithmetic  33.4 us (6%)
  matrix products  27.2 us (5%)
  waiting for transfers between devices  23.5 us (4%)
  between operations  11.2 us (2%)
    psum x3, blocking collectives, local(): lax.psum(jnp.sum(residual * residual, axis=0), ('cluster', 'sub'))  228 us
    psum x2, blocking collectives, local(): curvature = lax.psum(jnp.sum(direction * image, axis=0), ('cluster', 'sub'))  156 us
    ppermute x16, starting transfers between devices, passed_along(): return lax.ppermute(block, axis, route)  34.8 us
    dynamic_update_slice x12, local copies, waits for them, and re-layouts, insert_run(): lax.dynamic_update_slice_in_dim(padded, run_block, start_row, 0)[:dual_rows]  22.3 us
    ppermute x9, waiting for transfers between devices, added_up(): lax.ppermute(total, name, [(i, i ^ hop) for i in range(size)])  19.3 us
    dot_general x3, matrix products, local(): jnp.dot(operator, direction.astype(jnp.bfloat16), preferred_element_type=...  18.8 us
    ppermute x9, starting transfers between devices, added_up(): lax.ppermute(total, name, [(i, i ^ hop) for i in range(size)])  17.1 us
    another operation x12, local copies, waits for them, and re-layouts  14.4 us
  transfers between devices with their start and end apart: 25, of which 13 were waited for; matrix products, arithmetic and copies ran while one was open for 9% of the time, Pallas kernels for 0%

profile of v1, /device:TPU:1, one launch (start us, length us, event | category | flops | bytes accessed | tf_op | source)
XLA Modules:
  0.0 575.8 jit_solution(4800720229232982307)
XLA Ops:
  0.6 1.3 fusion.65
  8.5 1.2 constant_dynamic-slice_fusion.1
  10.5 1.2 iota_compare_fusion.6
  11.8 2.8 collective-permute-start.1
  16.4 4.8 collective-permute-start.3
  26.6 1.2 broadcast.85.clone.2
  27.8 1.8 dynamic_update_slice.49
  29.6 1.2 broadcast.85.clone.1
  30.8 1.9 dynamic_update_slice.50
  32.7 1.2 broadcast.85.clone
  33.9 1.8 dynamic_update_slice.51
  35.7 2.2 fusion.12
  39.5 2.9 collective-permute-done.4
  42.5 1.8 collective-permute-start.5
  44.2 3.0 collective-permute-done.5
  47.3 5.5 collective-permute-start.6
  52.8 2.3 collective-permute-done.6
  56.7 6.3 %fusion.6 = f32[128,2048]{1,0:T(8,128)S(1)} fusion(f32[128,2048]{1,0:T(8,128)S(1)} %fusion.34, bf16[1,1,2048,2048]{3,2,1,0:T(8,128)(2,1)} %param.6, f32[2048,128]{0,1:T(8,128)S(1)} %fusion.12), kind=kOutput, calls=%fused_computation.8 | convolution fusion | flops 1074266112 | bytes 11534336 | tf_op jit(solution)/shard_map/dot_general | solution.py:66
  64.1 5.1 collective-permute-start.8
  69.7 5.0 collective-permute-start.10
  74.7 1.2 broadcast.85.clone.5
  75.9 1.8 dynamic_update_slice.53
  78.1 1.2 broadcast.85.clone.4
  79.3 1.8 dynamic_update_slice.54
  81.1 1.2 broadcast.85.clone.3
  82.3 1.8 dynamic_update_slice.55
  84.2 2.8 multiply_reduce_fusion.4
  87.0 82.1 %all-reduce.4 = (f32[128]{0:T(128)S(1)}, f32[128]{0:T(128)S(1)}) all-reduce(f32[128]{0:T(128)} %get-tuple-element.5, f32[128]{0:T(128)} %get-tuple-element.4), channel_id=1, replica_groups=mesh['cluster'=8,'sub'=32] {'cluster','sub'}, use_global_device_ids=true, to_apply=%region_3.4 | all-reduce | flops 256 | bytes 2048 | tf_op jit(solution)/shard_map/psum | solution.py:64
  170.0 72.4 %psum.44 = f32[128]{0:T(128)S(1)} all-reduce(f32[128]{0:T(128)S(1)} %multiply_reduce_fusion.3), channel_id=1, replica_groups=mesh['cluster'=8,'sub'=32] {'cluster','sub'}, use_global_device_ids=true, to_apply=%region_7.8 | all-reduce | flops 128 | bytes 1024 | tf_op jit(solution)/shard_map/psum | solution.py:79
  245.3 1.9 collective-permute-start.11
  247.2 1.7 collective-permute-done.11
  249.1 3.9 collective-permute-done.12
  253.0 2.9 collective-permute-start.13
  255.9 6.2 %fusion.2 = f32[128,2048]{1,0:T(8,128)S(1)} fusion(bf16[1,1,2048,2048]{3,2,1,0:T(8,128)(2,1)} %param.6, f32[2048,128]{0,1:T(8,128)S(1)} %multiply_add_fusion.1), kind=kOutput, calls=%fused_computation.2 | convolution fusion | flops 1074003968 | bytes 10485760 | tf_op jit(solution)/shard_map/dot_general | solution.py:66
  264.9 3.6 collective-permute-start.15
  269.3 4.5 collective-permute-start.17
  273.8 1.2 broadcast.85.clone.8
  275.0 1.9 dynamic_update_slice.57
  278.5 1.9 dynamic_update_slice.58
  280.4 1.2 broadcast.85.clone.6
  281.6 1.9 dynamic_update_slice.59
  283.5 1.4 collective-permute-done.14
  284.9 4.2 multiply_reduce_fusion.2
  289.1 77.5 %psum.45 = f32[128]{0:T(128)} all-reduce(f32[128]{0:T(128)} %get-tuple-element.12), channel_id=1, replica_groups=mesh['cluster'=8,'sub'=32] {'cluster','sub'}, use_global_device_ids=true, to_apply=%region_9.10 | all-reduce | flops 128 | bytes 1024 | tf_op jit(solution)/shard_map/psum | solution.py:75
  367.2 3.0 multiply_reduce_fusion.1
  370.2 73.1 %psum.46 = f32[128]{0:T(128)S(1)} all-reduce(f32[128]{0:T(128)} %get-tuple-element.10), channel_id=1, replica_groups=mesh['cluster'=8,'sub'=32] {'cluster','sub'}, use_global_device_ids=true, to_apply=%region_11.12 | all-reduce | flops 128 | bytes 1024 | tf_op jit(solution)/shard_map/psum | solution.py:79
  444.0 1.4 multiply_add_fusion
  447.8 2.0 collective-permute-done.18
  450.5 3.5 collective-permute-done.19
  454.0 2.7 collective-permute-start.20
  456.8 6.2 %fusion = f32[128,2048]{1,0:T(8,128)S(1)} fusion(bf16[1,1,2048,2048]{3,2,1,0:T(8,128)(2,1)} %param.6, f32[2048,128]{0,1:T(8,128)S(1)} %multiply_add_fusion), kind=kOutput, calls=%fused_computation | convolution fusion | flops 1074003968 | bytes 10485760 | tf_op jit(solution)/shard_map/dot_general | solution.py:66
  465.8 3.5 collective-permute-start.22
  470.1 4.3 collective-permute-start.24
  474.4 1.2 broadcast.85.clone.11
  475.6 1.9 dynamic_update_slice.61
  479.3 1.9 dynamic_update_slice.62
  481.2 1.2 broadcast.85.clone.9
  482.4 1.9 dynamic_update_slice.63
  484.3 1.2 collective-permute-done.21
  485.5 3.7 multiply_reduce_fusion
  489.2 78.3 %psum.47 = f32[128]{0:T(128)} all-reduce(f32[128]{0:T(128)S(1)} %get-tuple-element.8), channel_id=1, replica_groups=mesh['cluster'=8,'sub'=32] {'cluster','sub'}, use_global_device_ids=true, to_apply=%region_13.14 | all-reduce | flops 128 | bytes 1024 | tf_op jit(solution)/shard_map/psum | solution.py:75
  568.2 3.3 subtract_bitcast_fusion
  571.5 2.6 copy.13
  574.1 1.3 copy.14
  (124 shorter events, 29.5 us)
Async XLA Ops:
  0.6 37.3 %copy-start = (f32[1,1,48,2048]{3,2,1,0:T(8,128)S(1)}, f32[1,1,48,2048]{3,2,1,0:T(8,128)}, u32[]{:S(2)}) copy-start(f32[1,1,48,2048]{3,2,1,0:T(8,128)} %param.7) | copy-start | bytes 1179652
  9.7 5.6 copy-start.4
  11.8 14.8 %collective-permute-start.1 = (f32[512,128]{0,1:T(8,128)S(1)}, f32[512,128]{0,1:T(8,128)S(1)}, u32[]{:S(2)}, u32[]{:S(2)}) collective-permute-start(f32[512,128]{0,1:T(8,128)S(1)} %bitcast_select_fusion.2), channel_id=1, source_target_pairs={{31,0},{0,1},{1,2},{2,3},{3,4},{4,5},{5,6},{6,7},{7,8},{8,9},{9,10... | collective-permute-start | bytes 786440 | tf_op jit(solution)/shard_map/ppermute | solution.py:24
  14.7 14.9 %collective-permute-start.2 = (f32[512,128]{0,1:T(8,128)S(1)}, f32[512,128]{0,1:T(8,128)}, u32[]{:S(2)}, u32[]{:S(2)}) collective-permute-start(f32[512,128]{0,1:T(8,128)S(1)} %bitcast_select_fusion.1), channel_id=1, source_target_pairs={{1,0},{2,1},{3,2},{4,3},{5,4},{6,5},{7,6},{8,7},{9,8},{10,9},{11,1... | collective-permute-start | bytes 786440 | tf_op jit(solution)/shard_map/ppermute | solution.py:24
  16.4 9.5 %copy-start.9 = (pred[512]{0:T(512)(128)(4,1)}, pred[512]{0:T(512)(128)(4,1)S(1)}, u32[]{:S(2)}) copy-start(pred[512]{0:T(512)(128)(4,1)S(1)} %iota_compare_fusion.5) | copy-start | bytes 1540
  16.4 16.3 %collective-permute-start.3 = (f32[512,128]{0,1:T(8,128)S(1)}, f32[512,128]{0,1:T(8,128)S(1)}, u32[]{:S(2)}, u32[]{:S(2)}) collective-permute-start(f32[512,128]{0,1:T(8,128)S(1)} %fusion.38), channel_id=1, source_target_pairs={{2,0},{3,1},{4,2},{5,3},{6,4},{7,5},{8,6},{9,7},{10,8},{11,9},{12,... | collective-permute-start | bytes 786440 | tf_op jit(solution)/shard_map/ppermute | solution.py:24
  22.0 8.8 %copy-start.13 = (pred[512]{0:T(512)(128)(4,1)}, pred[512]{0:T(512)(128)(4,1)S(1)}, u32[]{:S(2)}) copy-start(pred[512]{0:T(512)(128)(4,1)S(1)} %iota_compare_fusion.8) | copy-start | bytes 1540
  22.0 13.7 %collective-permute-start = (f32[512,128]{0,1:T(8,128)S(1)}, f32[512,128]{0,1:T(8,128)S(1)}, u32[]{:S(2)}, u32[]{:S(2)}) collective-permute-start(f32[512,128]{0,1:T(8,128)S(1)} %bitcast_select_fusion.3), channel_id=1, source_target_pairs={{30,0},{31,1},{0,2},{1,3},{2,4},{3,5},{4,6},{5,7},{6,8},{7,9},{8,1... | collective-permute-start | bytes 786440 | tf_op jit(solution)/shard_map/ppermute | solution.py:24
  37.9 1.0 copy-start.8
  37.9 17.2 %copy-start.5 = (f32[1,128,128]{2,1,0:T(8,128)S(1)}, f32[1,128,128]{2,1,0:T(8,128)}, u32[]{:S(2)}) copy-start(f32[1,128,128]{2,1,0:T(8,128)} %param.8) | copy-start | bytes 196612
  39.2 3.2 collective-permute-start.4
  42.5 4.8 collective-permute-start.5
  47.3 7.9 %collective-permute-start.6 = (f32[128,128]{1,0:T(8,128)S(1)}, f32[128,128]{1,0:T(8,128)S(1)}, u32[]{:S(2)}, u32[]{:S(2)}) collective-permute-start(f32[128,128]{1,0:T(8,128)S(1)} %add.172), channel_id=1, source_target_pairs={{0,128},{32,160},{64,192},{96,224},{128,0},{160,32},{192,64},{224,... | collective-permute-start | bytes 196616 | tf_op jit(solution)/shard_map/ppermute | solution.py:16
  56.7 6.3 %copy-start.14 = (pred[512]{0:T(512)(128)(4,1)S(1)}, pred[512]{0:T(512)(128)(4,1)}, u32[]{:S(2)}) copy-start(pred[512]{0:T(512)(128)(4,1)} %copy-done.13) | copy-start | bytes 1540
  63.0 6.7 %copy-start.10 = (pred[512]{0:T(512)(128)(4,1)S(1)}, pred[512]{0:T(512)(128)(4,1)}, u32[]{:S(2)}) copy-start(pred[512]{0:T(512)(128)(4,1)} %copy-done.9) | copy-start | bytes 1540
  64.1 10.6 %collective-permute-start.8 = (f32[512,128]{0,1:T(8,128)S(1)}, f32[512,128]{0,1:T(8,128)S(1)}, u32[]{:S(2)}, u32[]{:S(2)}) collective-permute-start(f32[512,128]{0,1:T(8,128)S(1)} %get-tuple-element.23), channel_id=1, source_target_pairs={{31,0},{0,1},{1,2},{2,3},{3,4},{4,5},{5,6},{6,7},{7,8},{8,9},{9,10... | collective-permute-start | bytes 786440 | tf_op jit(solution)/shard_map/ppermute | solution.py:24
  69.2 8.9 %collective-permute-start.9 = (f32[512,128]{0,1:T(8,128)}, f32[512,128]{0,1:T(8,128)S(1)}, u32[]{:S(2)}, u32[]{:S(2)}) collective-permute-start(f32[512,128]{0,1:T(8,128)} %get-tuple-element.22), channel_id=1, source_target_pairs={{1,0},{2,1},{3,2},{4,3},{5,4},{6,5},{7,6},{8,7},{9,8},{10,9},{11,1... | collective-permute-start | bytes 786440 | tf_op jit(solution)/shard_map/ppermute | solution.py:24
  69.7 11.4 %collective-permute-start.10 = (f32[512,128]{0,1:T(8,128)S(1)}, f32[512,128]{0,1:T(8,128)S(1)}, u32[]{:S(2)}, u32[]{:S(2)}) collective-permute-start(f32[512,128]{0,1:T(8,128)S(1)} %slice_select_fusion.2), channel_id=1, source_target_pairs={{2,0},{3,1},{4,2},{5,3},{6,4},{7,5},{8,6},{9,7},{10,8},{11,9},{12,... | collective-permute-start | bytes 786440 | tf_op jit(solution)/shard_map/ppermute | solution.py:24
  74.7 9.6 %collective-permute-start.7 = (f32[512,128]{0,1:T(8,128)}, f32[512,128]{0,1:T(8,128)}, u32[]{:S(2)}, u32[]{:S(2)}) collective-permute-start(f32[512,128]{0,1:T(8,128)} %get-tuple-element.21), channel_id=1, source_target_pairs={{30,0},{31,1},{0,2},{1,3},{2,4},{3,5},{4,6},{5,7},{6,8},{7,9},{8,1... | collective-permute-start | bytes 786440 | tf_op jit(solution)/shard_map/ppermute | solution.py:24
  169.2 0.6 copy-start.17
  242.5 0.6 copy-start.22
  245.3 3.5 collective-permute-start.11
  248.8 4.1 collective-permute-start.12
  252.9 9.2 %copy-start.6 = (f32[1,128,128]{2,1,0:T(8,128)S(1)}, f32[1,128,128]{2,1,0:T(8,128)}, u32[]{:S(2)}) copy-start(f32[1,128,128]{2,1,0:T(8,128)} %param.8) | copy-start | bytes 196612
  253.0 9.2 %collective-permute-start.13 = (f32[128,128]{1,0:T(8,128)S(1)}, f32[128,128]{1,0:T(8,128)S(1)}, u32[]{:S(2)}, u32[]{:S(2)}) collective-permute-start(f32[128,128]{1,0:T(8,128)S(1)} %add.182), channel_id=1, source_target_pairs={{0,128},{32,160},{64,192},{96,224},{128,0},{160,32},{192,64},{224,... | collective-permute-start | bytes 196616 | tf_op jit(solution)/shard_map/ppermute | solution.py:16
  262.4 1.3 copy-start.15
  263.8 4.8 copy-start.2
  263.8 4.8 copy-start.11
  264.9 8.9 %collective-permute-start.15 = (f32[512,128]{0,1:T(8,128)S(1)}, f32[512,128]{0,1:T(8,128)}, u32[]{:S(2)}, u32[]{:S(2)}) collective-permute-start(f32[512,128]{0,1:T(8,128)S(1)} %get-tuple-element.20), channel_id=1, source_target_pairs={{31,0},{0,1},{1,2},{2,3},{3,4},{4,5},{5,6},{6,7},{7,8},{8,9},{9,10... | collective-permute-start | bytes 786440 | tf_op jit(solution)/shard_map/ppermute | solution.py:24
  268.5 8.8 %collective-permute-start.16 = (f32[512,128]{0,1:T(8,128)}, f32[512,128]{0,1:T(8,128)}, u32[]{:S(2)}, u32[]{:S(2)}) collective-permute-start(f32[512,128]{0,1:T(8,128)} %get-tuple-element.19), channel_id=1, source_target_pairs={{1,0},{2,1},{3,2},{4,3},{5,4},{6,5},{7,6},{8,7},{9,8},{10,9},{11,1... | collective-permute-start | bytes 786440 | tf_op jit(solution)/shard_map/ppermute | solution.py:24
  269.3 11.1 %collective-permute-start.17 = (f32[512,128]{0,1:T(8,128)}, f32[512,128]{0,1:T(8,128)}, u32[]{:S(2)}, u32[]{:S(2)}) collective-permute-start(f32[512,128]{0,1:T(8,128)} %slice_select_fusion.1), channel_id=1, source_target_pairs={{2,0},{3,1},{4,2},{5,3},{6,4},{7,5},{8,6},{9,7},{10,8},{11,9},{12,... | collective-permute-start | bytes 786440 | tf_op jit(solution)/shard_map/ppermute | solution.py:24
  273.8 11.1 %collective-permute-start.14 = (f32[512,128]{0,1:T(8,128)}, f32[512,128]{0,1:T(8,128)}, u32[]{:S(2)}, u32[]{:S(2)}) collective-permute-start(f32[512,128]{0,1:T(8,128)} %get-tuple-element.18), channel_id=1, source_target_pairs={{30,0},{31,1},{0,2},{1,3},{2,4},{3,5},{4,6},{5,7},{6,8},{7,9},{8,1... | collective-permute-start | bytes 786440 | tf_op jit(solution)/shard_map/ppermute | solution.py:24
  367.2 3.0 copy-start.19
  443.3 0.7 copy-start.21
  446.7 3.2 collective-permute-start.18
  449.9 4.1 collective-permute-start.19
  454.0 9.0 %copy-start.7 = (f32[1,128,128]{2,1,0:T(8,128)S(1)}, f32[1,128,128]{2,1,0:T(8,128)}, u32[]{:S(2)}) copy-start(f32[1,128,128]{2,1,0:T(8,128)} %param.8) | copy-start | bytes 196612
  454.0 9.0 %collective-permute-start.20 = (f32[128,128]{1,0:T(8,128)S(1)}, f32[128,128]{1,0:T(8,128)S(1)}, u32[]{:S(2)}, u32[]{:S(2)}) collective-permute-start(f32[128,128]{1,0:T(8,128)S(1)} %add.193), channel_id=1, source_target_pairs={{0,128},{32,160},{64,192},{96,224},{128,0},{160,32},{192,64},{224,... | collective-permute-start | bytes 196616 | tf_op jit(solution)/shard_map/ppermute | solution.py:16
  463.3 1.3 copy-start.16
  464.6 4.7 copy-start.1
  464.7 4.7 copy-start.12
  465.8 8.6 %collective-permute-start.22 = (f32[512,128]{0,1:T(8,128)S(1)}, f32[512,128]{0,1:T(8,128)}, u32[]{:S(2)}, u32[]{:S(2)}) collective-permute-start(f32[512,128]{0,1:T(8,128)S(1)} %get-tuple-element.17), channel_id=1, source_target_pairs={{31,0},{0,1},{1,2},{2,3},{3,4},{4,5},{5,6},{6,7},{7,8},{8,9},{9,10... | collective-permute-start | bytes 786440 | tf_op jit(solution)/shard_map/ppermute | solution.py:24
  469.3 8.8 %collective-permute-start.23 = (f32[512,128]{0,1:T(8,128)}, f32[512,128]{0,1:T(8,128)}, u32[]{:S(2)}, u32[]{:S(2)}) collective-permute-start(f32[512,128]{0,1:T(8,128)} %get-tuple-element.16), channel_id=1, source_target_pairs={{1,0},{2,1},{3,2},{4,3},{5,4},{6,5},{7,6},{8,7},{9,8},{10,9},{11,1... | collective-permute-start | bytes 786440 | tf_op jit(solution)/shard_map/ppermute | solution.py:24
  470.1 11.1 %collective-permute-start.24 = (f32[512,128]{0,1:T(8,128)}, f32[512,128]{0,1:T(8,128)}, u32[]{:S(2)}, u32[]{:S(2)}) collective-permute-start(f32[512,128]{0,1:T(8,128)} %slice_select_fusion), channel_id=1, source_target_pairs={{2,0},{3,1},{4,2},{5,3},{6,4},{7,5},{8,6},{9,7},{10,8},{11,9},{12,... | collective-permute-start | bytes 786440 | tf_op jit(solution)/shard_map/ppermute | solution.py:24
  474.4 11.1 %collective-permute-start.21 = (f32[512,128]{0,1:T(8,128)}, f32[512,128]{0,1:T(8,128)}, u32[]{:S(2)}, u32[]{:S(2)}) collective-permute-start(f32[512,128]{0,1:T(8,128)} %get-tuple-element.15), channel_id=1, source_target_pairs={{30,0},{31,1},{0,2},{1,3},{2,4},{3,5},{4,6},{5,7},{6,8},{7,9},{8,1... | collective-permute-start | bytes 786440 | tf_op jit(solution)/shard_map/ppermute | solution.py:24
  484.3 83.9 %copy-start.18 = (f32[128]{0:T(128)S(1)}, f32[128]{0:T(128)}, u32[]{:S(2)}) copy-start(f32[128]{0:T(128)} %copy-done.17) | copy-start | bytes 1540
  484.3 83.9 %copy-start.20 = (f32[128]{0:T(128)S(1)}, f32[128]{0:T(128)}, u32[]{:S(2)}) copy-start(f32[128]{0:T(128)} %copy-done.19) | copy-start | bytes 1540
  571.5 2.6 copy-start.3
